TPU v7x, 256 devices: a whole 4x4x8 slice. The times are simulated.
256 devices in a mesh: chan: 8 (over z_lo, core), region: 32 (over x, y, z_hi).
Axes of the slice: x: 4, y: 4, z: 8 (z_hi: 2, z_lo: 4; z = z_hi * 4 + z_lo), core: 2. Of those that a mesh axis runs over, the one named last changes fastest.
Arguments:
- latent: bfloat16 [32, 24, 24, 12, 128], P('region'), may hold values from -6 to 6
- cond_scale: float32 [128], replicated, may hold values from 0.5 to 1.5
- cond_shift: float32 [128], replicated, may hold values from -3 to 3
- fine_weight: bfloat16 [3, 3, 3, 128, 128], replicated, may hold values from -0.109375 to 0.109375
- fine_bias: float32 [128], replicated, may hold values from -3 to 3
- proj_weight: bfloat16 [8192, 1024], P(('chan', 'region')), may hold values from -0.0625 to 0.0625
- proj_bias: float32 [1024], replicated, may hold values from -3 to 3
- bottle_weight: bfloat16 [27, 1024, 1024], P(None, 'chan'), may hold values from -0.0390625 to 0.0390625
- bottle_bias: float32 [1024], replicated, may hold values from -3 to 3
- guide: float32 [1], replicated, may hold values from 1.5 to 4
Outputs:
- guided: bfloat16 [32, 6, 6, 3, 1024], P('region', None, None, None, 'chan')
All inputs are finite; a program needn't handle non-finite values.
Results may differ from a plain program's by a relative error of at most 0.012.
The roundings to bfloat16 on the way count: a program that leaves them out, or rounds other values in their place, can miss the bound.
Values may be sent and summed in bfloat16 or wider, within the bound.
A program may use at most 128 MiB of HBM per device.

v0:
```python
import jax
import jax.numpy as jnp
from jax import lax
from jax.sharding import PartitionSpec as P

FINE_WIDTH = 128
COARSE_WIDTH = 1024
TILE_SIDE = 12
STRIDE = 4
REGIONS_Y = 4
REGIONS_Z = 2


def passed_along(value, axis, steps):
    count = lax.axis_size(axis)
    leading, last = (max(0, -steps), min(count, count - steps))
    return lax.ppermute(value, axis, [(source, source + steps) for source in range(leading, last)])


def extend(block, axis_dim, stride, count):
    place = lax.axis_index("region") // stride % count
    length = block.shape[axis_dim]
    last_layer = lax.slice_in_dim(block, length - 1, length, axis=axis_dim)
    first_layer = lax.slice_in_dim(block, 0, 1, axis=axis_dim)
    arrived = [
        passed_along(layer, "region", offset)
        for layer, offset in ((last_layer, stride), (first_layer, -stride))
    ]
    below = jnp.where(place > 0, arrived[0], jnp.zeros_like(arrived[0]))
    above = jnp.where(place < count - 1, arrived[1], jnp.zeros_like(arrived[1]))
    return jnp.concatenate([below, block, above], axis=axis_dim)


def surround(block, lead):
    count_x = lax.axis_size("region") // (REGIONS_Y * REGIONS_Z)
    block = extend(block, lead + 2, 1, REGIONS_Z)
    block = extend(block, lead + 1, REGIONS_Z, REGIONS_Y)
    return extend(block, lead, REGIONS_Y * REGIONS_Z, count_x)


def fine_conv(window, weight, bias, side):
    stacked = jnp.concatenate(
        [
            window[step_x : step_x + side, step_y : step_y + side, step_z : step_z + side]
            for step_x in range(3)
            for step_y in range(3)
            for step_z in range(3)
        ],
        axis=3,
    )
    stacked = stacked.reshape(side**3, -1)
    total = jnp.dot(
        stacked, weight.reshape(-1, weight.shape[4]), preferred_element_type=jnp.float32
    )
    return jax.nn.silu(total + bias).astype(jnp.bfloat16).reshape(side, side, side, -1)


def to_patches(tile, side):
    cells = side // STRIDE
    grid = tile.reshape(cells, STRIDE, cells, STRIDE, cells, STRIDE, tile.shape[3])
    grid = grid.transpose(0, 2, 4, 6, 1, 3, 5)
    return grid.reshape(cells**3, tile.shape[3] * STRIDE**3)


def shards(
    latent,
    cond_scale,
    cond_shift,
    fine_weight,
    fine_bias,
    proj_weight,
    proj_bias,
    bottle_weight,
    bottle_bias,
    guide,
):
    side = TILE_SIDE
    cells = side // STRIDE
    channels = lax.axis_size("chan")
    chan_place = lax.axis_index("chan")
    per_copy = channels // 2
    tiles_dev = 8 // channels
    copy_index = chan_place // per_copy
    first_tile = chan_place % per_copy * tiles_dev
    width = COARSE_WIDTH // channels
    depth = FINE_WIDTH * STRIDE**3
    block = latent[0].astype(jnp.float32)
    shaped = block * cond_scale + cond_shift
    source = jnp.where(copy_index == 1, shaped, block).astype(jnp.bfloat16)
    padded = surround(source, 0)
    patches = []
    which = first_tile + 0
    window = lax.dynamic_slice(
        padded,
        (which // 2 * side, which % 2 * side, 0, 0),
        (side + 2, side + 2, side + 2, FINE_WIDTH),
    )
    patches.append(to_patches(fine_conv(window, fine_weight, fine_bias, side), side))
    patches = jnp.stack(patches)
    flat = patches.reshape(tiles_dev * cells**3, depth)
    summed = jnp.dot(
        flat,
        lax.all_gather(proj_weight, ("chan", "region"), axis=0, tiled=True),
        preferred_element_type=jnp.float32,
    )
    projected = (summed + proj_bias).astype(jnp.bfloat16)
    coarse = lax.all_to_all(projected, "chan", split_axis=1, concat_axis=0, tiled=True)
    grid = coarse.reshape(2, 2, 2, cells, cells, cells, width).transpose(0, 1, 3, 2, 4, 5, 6)
    grid = grid.reshape(2, 2 * cells, 2 * cells, cells, width)
    framed = surround(grid, 1)
    stacked = jnp.concatenate(
        [
            framed[
                :, step_x : step_x + 2 * cells, step_y : step_y + 2 * cells, step_z : step_z + cells
            ]
            for step_x in range(3)
            for step_y in range(3)
            for step_z in range(3)
        ],
        axis=4,
    )
    stacked = stacked.reshape(-1, 27 * width)
    terms = jnp.dot(
        stacked, bottle_weight.reshape(27 * width, COARSE_WIDTH), preferred_element_type=jnp.float32
    )
    summed = lax.psum_scatter(terms, "chan", scatter_dimension=1, tiled=True)
    bottle = jax.nn.silu(summed + lax.dynamic_slice_in_dim(bottle_bias, chan_place * width, width))
    bottle = bottle.reshape(2, 2 * cells, 2 * cells, cells, width)
    guided = (bottle[0] + guide[0] * (bottle[1] - bottle[0])).astype(jnp.bfloat16)
    return guided[None]


def solution(mesh):
    placed = (
        P("region", None, None, None, None),
        P(),
        P(),
        P(),
        P(),
        P(("chan", "region"), None),
        P(),
        P(None, "chan", None),
        P(),
        P(),
    )
    return jax.shard_map(
        shards,
        mesh=mesh,
        in_specs=placed,
        out_specs=P("region", None, None, None, "chan"),
        check_vma=False,
    )
```

profile of v0, /device:TPU:2, one launch (start us, length us, event | category | flops | bytes accessed | tf_op | source)
XLA Modules:
  0.0 859.1 jit_solution(12610991419264779117)
XLA Ops:
  7.3 2.1 fusion.1
  9.4 9.1 %collective-permute-start = (bf16[24,24,1,128]{3,1,2,0:T(8,128)(2,1)S(1)}, bf16[24,24,1,128]{3,1,2,0:T(8,128)(2,1)S(1)}, u32[]{:S(2)}, u32[]{:S(2)}) collective-permute-start(bf16[24,24,1,128]{3,1,2,0:T(8,128)(2,1)S(1)} %get-tuple-element.9), channel_id=1, source_target_pairs={{0,1},{1,2},{2,3},{3,4},{4,5},{5,6},{6,7},{7,8},{8,9},{9,10},{10,1... | collective-permute-start | bytes 442376 | tf_op jit(solution)/shard_map/ppermute | solution.py:17
  18.5 4.3 collective-permute-start.1
  24.9 10.2 %collective-permute-done.1 = bf16[24,24,1,128]{3,1,2,0:T(8,128)(2,1)S(1)} collective-permute-done((bf16[24,24,1,128]{3,1,2,0:T(8,128)(2,1)S(1)}, bf16[24,24,1,128]{3,1,2,0:T(8,128)(2,1)S(1)}, u32[]{:S(2)}, u32[]{:S(2)}) %collective-permute-start.1) | collective-permute-done | bytes 147488 | tf_op jit(solution)/shard_map/ppermute | solution.py:17
  35.4 3.4 collective-permute-start.2
  38.8 4.6 collective-permute-start.3
  43.4 2.0 collective-permute-done.2
  47.4 2.9 collective-permute-start.5
  50.4 3.1 collective-permute-start.4
  54.4 2.7 collective-permute-done.4
  67.1 9.4 %copy.70 = bf16[12,12,12,3456]{3,2,1,0:T(8,128)(2,1)} copy(bf16[12,12,12,3456]{3,1,2,0:T(8,128)(2,1)S(1)} %slice_dynamic-update-slice_fusion) | data formatting | bytes 23887872 | tf_op jit(solution)/shard_map/concatenate | solution.py:42
  76.5 18.7 %reshape.92 = bf16[1728,3456]{1,0:T(8,128)(2,1)} reshape(bf16[12,12,12,3456]{3,2,1,0:T(8,128)(2,1)} %copy.70) | data formatting | bytes 23887872 | tf_op jit(solution)/shard_map/reshape | solution.py:51
  95.2 7.7 multiply_convert_fusion
  102.9 17.5 %copy.71 = bf16[3,4,3,4,3,4,128]{5,3,1,6,4,2,0:T(4,128)(2,1)} copy(bf16[3,4,3,4,3,4,128]{6,5,4,3,2,1,0:T(4,128)(2,1)S(1)} %bitcast.33) | data formatting | bytes 884736 | tf_op jit(solution)/shard_map/reshape;reshape | solution.py:60
  120.4 37.1 %reshape_stack_reshape.3 = bf16[27,8192]{1,0:T(8,128)(2,1)S(1)} reshape(bf16[3,3,3,128,4,4,4]{6,5,4,3,2,1,0:T(4,128)(2,1)} %bitcast.24) | data formatting | bytes 884736 | tf_op jit(solution)/shard_map/reshape;stack;reshape | solution.py:100
  157.5 585.9 %all-gather.2.cloned.1.call-done = bf16[8192,1024]{1,0:T(8,128)(2,1)} async-done(((bf16[32,1024]{1,0:T(8,128)(2,1)}), bf16[8192,1024]{1,0:T(8,128)(2,1)}) %all-gather.2.cloned.1.call-update) | async-done | bytes 16777232 | tf_op jit(solution)/shard_map/all_gather | solution.py:103
  743.4 8.8 %fusion.2 = bf16[27,1024]{1,0:T(8,128)(2,1)S(1)} fusion(bf16[27,8192]{1,0:T(8,128)(2,1)S(1)} %reshape_stack_reshape.3, bf16[8192,1024]{1,0:T(8,128)(2,1)} %all-gather.2.cloned.1.call-done, f32[1024]{0:T(1024)S(1)} %copy-done.2), kind=kOutput, calls=%fused_computation.13 | convolution fusion | flops 453040128 | bytes 17278976 | tf_op jit(solution)/shard_map/dot_general | solution.py:101
  752.2 19.5 %all_to_all.16 = bf16[27,8,128]{2,0,1:T(8,128)(2,1)S(1)} all-to-all(bf16[27,8,128]{2,0,1:T(8,128)(2,1)S(1)} %copy.72), channel_id=1, replica_groups=mesh['chan'=8,'region'=32] {'chan'}, dimensions={1} | all-to-all | bytes 110592 | tf_op jit(solution)/shard_map/all_to_all | solution.py:107
  771.8 3.2 collective-permute-start.6
  775.1 9.8 %collective-permute-start.7 = (bf16[2,6,6,1,128]{4,0,3,2,1:T(2,128)(2,1)S(1)}, bf16[2,6,6,1,128]{4,0,3,2,1:T(2,128)(2,1)S(1)}, u32[]{:S(2)}, u32[]{:S(2)}) collective-permute-start(bf16[2,6,6,1,128]{4,0,3,2,1:T(2,128)(2,1)S(1)} %get-tuple-element.48), channel_id=1, source_target_pairs={{1,0},{2,1},{3,2},{4,3},{5,4},{6,5},{7,6},{8,7},{9,8},{10,9},{11,1... | collective-permute-start | bytes 55304 | tf_op jit(solution)/shard_map/ppermute | solution.py:17
  788.6 6.0 collective-permute-start.9
  798.7 3.9 collective-permute-start.11
  807.6 5.8 fusion.16
  814.8 35.8 %reduce-scatter.2.cloned.1.call-done = f32[216,128]{1,0:T(8,128)} async-done(((f32[216,1024]{1,0:T(8,128)}), f32[216,128]{1,0:T(8,128)}) %reduce-scatter.2.cloned.1.call-update) | async-done | bytes 110608 | tf_op jit(solution)/shard_map/reduce_scatter | solution.py:126
  (166 shorter events, 30.5 us)
Async XLA Ops:
  6.5 88.6 %copy-start = (bf16[3,3,3,128,128]{4,3,2,1,0:T(8,128)(2,1)S(1)}, bf16[3,3,3,128,128]{4,3,2,1,0:T(8,128)(2,1)}, u32[]{:S(2)}) copy-start(bf16[3,3,3,128,128]{4,3,2,1,0:T(8,128)(2,1)} %param.13) | copy-start | bytes 2654212
  6.5 736.9 %all-gather.2.cloned.1.call-start = ((), (), s32[]{:S(2)}) async-start(), calls=%async_computation.2 | async-start | bytes 16842752 | tf_op jit(solution)/shard_map/all_gather | solution.py:103
  7.3 843.3 %reduce-scatter.2.cloned.1.call-start = ((), (), s32[]{:S(2)}) async-start(), calls=%async_computation.3 | async-start | bytes 995328 | tf_op jit(solution)/shard_map/reduce_scatter | solution.py:126
  9.4 15.5 %collective-permute-start = (bf16[24,24,1,128]{3,1,2,0:T(8,128)(2,1)S(1)}, bf16[24,24,1,128]{3,1,2,0:T(8,128)(2,1)S(1)}, u32[]{:S(2)}, u32[]{:S(2)}) collective-permute-start(bf16[24,24,1,128]{3,1,2,0:T(8,128)(2,1)S(1)} %get-tuple-element.9), channel_id=1, source_target_pairs={{0,1},{1,2},{2,3},{3,4},{4,5},{5,6},{6,7},{7,8},{8,9},{9,10},{10,1... | collective-permute-start | bytes 442376 | tf_op jit(solution)/shard_map/ppermute | solution.py:17
  18.5 16.5 %collective-permute-start.1 = (bf16[24,24,1,128]{3,1,2,0:T(8,128)(2,1)S(1)}, bf16[24,24,1,128]{3,1,2,0:T(8,128)(2,1)S(1)}, u32[]{:S(2)}, u32[]{:S(2)}) collective-permute-start(bf16[24,24,1,128]{3,1,2,0:T(8,128)(2,1)S(1)} %get-tuple-element.10), channel_id=1, source_target_pairs={{1,0},{2,1},{3,2},{4,3},{5,4},{6,5},{7,6},{8,7},{9,8},{10,9},{11,1... | collective-permute-start | bytes 442376 | tf_op jit(solution)/shard_map/ppermute | solution.py:17
  35.4 10.0 %collective-permute-start.2 = (bf16[24,1,14,128]{3,1,2,0:T(2,128)(2,1)S(1)}, bf16[24,1,14,128]{3,1,2,0:T(2,128)(2,1)S(1)}, u32[]{:S(2)}, u32[]{:S(2)}) collective-permute-start(bf16[24,1,14,128]{3,1,2,0:T(2,128)(2,1)S(1)} %get-tuple-element.7), channel_id=1, source_target_pairs={{0,2},{1,3},{2,4},{3,5},{4,6},{5,7},{6,8},{7,9},{8,10},{9,11},{10,... | collective-permute-start | bytes 258056 | tf_op jit(solution)/shard_map/ppermute | solution.py:17
  38.8 7.7 collective-permute-start.3
  47.4 7.0 collective-permute-start.5
  50.4 6.8 collective-permute-start.4
  76.5 18.7 %copy-start.3 = (f32[128]{0:T(128)S(1)}, f32[128]{0:T(128)}, u32[]{:S(2)}) copy-start(f32[128]{0:T(128)} %param.14) | copy-start | bytes 1540
  120.4 623.0 %copy-start.2 = (f32[1024]{0:T(1024)S(1)}, f32[1024]{0:T(1024)}, u32[]{:S(2)}) copy-start(f32[1024]{0:T(1024)} %param.16) | copy-start | bytes 12292
  771.8 13.1 %collective-permute-start.6 = (bf16[2,6,6,1,128]{4,0,3,2,1:T(2,128)(2,1)S(1)}, bf16[2,6,6,1,128]{4,0,3,2,1:T(2,128)(2,1)S(1)}, u32[]{:S(2)}, u32[]{:S(2)}) collective-permute-start(bf16[2,6,6,1,128]{4,0,3,2,1:T(2,128)(2,1)S(1)} %get-tuple-element.47), channel_id=1, source_target_pairs={{0,1},{1,2},{2,3},{3,4},{4,5},{5,6},{6,7},{7,8},{8,9},{9,10},{10,1... | collective-permute-start | bytes 55304 | tf_op jit(solution)/shard_map/ppermute | solution.py:17
  775.1 11.2 %collective-permute-start.7 = (bf16[2,6,6,1,128]{4,0,3,2,1:T(2,128)(2,1)S(1)}, bf16[2,6,6,1,128]{4,0,3,2,1:T(2,128)(2,1)S(1)}, u32[]{:S(2)}, u32[]{:S(2)}) collective-permute-start(bf16[2,6,6,1,128]{4,0,3,2,1:T(2,128)(2,1)S(1)} %get-tuple-element.48), channel_id=1, source_target_pairs={{1,0},{2,1},{3,2},{4,3},{5,4},{6,5},{7,6},{8,7},{9,8},{10,9},{11,1... | collective-permute-start | bytes 55304 | tf_op jit(solution)/shard_map/ppermute | solution.py:17
  786.4 8.3 collective-permute-start.8
  788.6 7.5 collective-permute-start.9
  796.5 6.6 collective-permute-start.10
  798.7 5.7 collective-permute-start.11
  807.6 44.7 %copy-start.1 = (bf16[3,3,3,128,128]{4,3,2,1,0:T(8,128)(2,1)S(1)}, bf16[3,3,3,128,128]{4,3,2,1,0:T(8,128)(2,1)}, u32[]{:S(2)}) copy-start(bf16[3,3,3,128,128]{4,3,2,1,0:T(8,128)(2,1)} %param.13) | copy-start | bytes 2654212
Sparse Core Ops, SparseCore 0:
  9.2 734.1 all-gather.1
  813.5 37.0 reduce-scatter.1
where the time goes:
time: 860 us; the launch traced here: 859 us
  waiting for transfers between devices  645 us (75%)
  local copies, waits for them, and re-layouts  94.7 us (11%)
  starting transfers between devices  54.3 us (6%)
  matrix products  22.3 us (3%)
  blocking collectives  19.5 us (2%)
  between operations  15.2 us (2%)
    all_gather x1, waiting for transfers between devices, shards(): lax.all_gather(proj_weight, ('chan', 'region'), axis=0, tiled=True)  586 us
    ppermute x12, starting transfers between devices, passed_along(): lax.ppermute(value, axis, [(source, source + steps) for source in range(l...  54.2 us
    another operation x1, local copies, waits for them, and re-layouts, shards(): flat = patches.reshape(tiles_dev * cells ** 3, depth)  37.1 us
    reduce_scatter x1, waiting for transfers between devices, shards(): summed = lax.psum_scatter(terms, 'chan', scatter_dimension=1, tiled=True)  35.8 us
    ppermute x12, waiting for transfers between devices, passed_along(): lax.ppermute(value, axis, [(source, source + steps) for source in range(l...  22.6 us
    all_to_all x1, blocking collectives, shards(): lax.all_to_all(projected, 'chan', split_axis=1, concat_axis=0, tiled=True)  19.5 us
    reshape x1, local copies, waits for them, and re-layouts, fine_conv(): stacked = stacked.reshape(side ** 3, -1)  18.7 us
    another operation x1, local copies, waits for them, and re-layouts, to_patches(): tile.reshape(cells, STRIDE, cells, STRIDE, cells, STRIDE, tile.shape[3])  17.5 us
  transfers between devices with their start and end apart: 14, of which 11 were waited for; matrix products, arithmetic and copies ran while one was open for 12% of the time, Pallas kernels for 0%

commit v1 on v0

--- a/solution.py
+++ b/solution.py
@@ -9,6 +9,13 @@
 STRIDE = 4
 REGIONS_Y = 4
 REGIONS_Z = 2
+
+
+def all_by_exchange(block, mesh_axis, dim):
+    count = lax.axis_size(mesh_axis)
+    blocks = jnp.stack([block for _ in range(count)])
+    blocks = lax.all_to_all(blocks, mesh_axis, split_axis=0, concat_axis=0)
+    return jnp.concatenate(blocks, axis=dim)
 
 
 def passed_along(value, axis, steps):
@@ -100,7 +107,7 @@
     flat = patches.reshape(tiles_dev * cells**3, depth)
     summed = jnp.dot(
         flat,
-        lax.all_gather(proj_weight, ("chan", "region"), axis=0, tiled=True),
+        all_by_exchange(proj_weight, ("chan", "region"), 0),
         preferred_element_type=jnp.float32,
     )
     projected = (summed + proj_bias).astype(jnp.bfloat16)

time: 860 us -> 651 us (0.76)
  waiting for transfers between devices: 645 us -> 410 us
  local copies, waits for them, and re-layouts: 94.7 us -> 112 us
  starting transfers between devices: 54.3 us -> 69.4 us
  blocking collectives: 19.5 us -> 9.04 us
    all_gather x1 -> x0, waiting for transfers between devices: 586 us -> none  [shards(): lax.all_gather(proj_weight, ('chan', 'region'), axis=0, tiled=True)]
    ppermute x12, waiting for transfers between devices: 22.6 us -> 373 us  [passed_along(): lax.ppermute(value, axis, [(source, source + steps) for source in range(l...]
    all_to_all x0 -> x1, starting transfers between devices: none -> 15.7 us  [all_by_exchange(): blocks = lax.all_to_all(blocks, mesh_axis, split_axis=0, concat_axis=0)]
    concatenate x2, local copies, waits for them, and re-layouts: 9.68 us -> 20.8 us  [fine_conv(): jnp.concatenate([window[step_x:step_x + side, step_y:step_y + side, step_...]
    all_to_all x1, blocking collectives: 19.5 us -> 9.04 us  [shards(): lax.all_to_all(projected, 'chan', split_axis=1, concat_axis=0, tiled=True)]
  transfers between devices with their start and end apart: 14 -> 14, of which waited for: 11 -> 10; matrix products, arithmetic and copies ran while one was open for 12% -> 18% of each run, Pallas kernels for 0% -> 0%
where the time goes in v1:
time: 651 us; the launch traced here: 646 us
  waiting for transfers between devices  410 us (63%)
  local copies, waits for them, and re-layouts  112 us (17%)
  starting transfers between devices  69.4 us (11%)
  matrix products  22.2 us (3%)
  between operations  15.5 us (2%)
  blocking collectives  9.04 us (1%)
  other arithmetic  8.17 us (1%)
    ppermute x12, waiting for transfers between devices, passed_along(): lax.ppermute(value, axis, [(source, source + steps) for source in range(l...  373 us
    ppermute x12, starting transfers between devices, passed_along(): lax.ppermute(value, axis, [(source, source + steps) for source in range(l...  53.6 us
    another operation x1, local copies, waits for them, and re-layouts, shards(): flat = patches.reshape(tiles_dev * cells ** 3, depth)  37.1 us
    reduce_scatter x1, waiting for transfers between devices, shards(): summed = lax.psum_scatter(terms, 'chan', scatter_dimension=1, tiled=True)  36.9 us
    concatenate x2, local copies, waits for them, and re-layouts, fine_conv(): jnp.concatenate([window[step_x:step_x + side, step_y:step_y + side, step_...  20.8 us
    reshape x1, local copies, waits for them, and re-layouts, fine_conv(): stacked = stacked.reshape(side ** 3, -1)  18.6 us
    another operation x1, local copies, waits for them, and re-layouts, to_patches(): tile.reshape(cells, STRIDE, cells, STRIDE, cells, STRIDE, tile.shape[3])  17.3 us
    all_to_all x1, starting transfers between devices, all_by_exchange(): blocks = lax.all_to_all(blocks, mesh_axis, split_axis=0, concat_axis=0)  15.7 us
  transfers between devices with their start and end apart: 14, of which 10 were waited for; matrix products, arithmetic and copies ran while one was open for 18% of the time, Pallas kernels for 0%

profile of v1, /device:TPU:2, one launch (start us, length us, event | category | flops | bytes accessed | tf_op | source)
XLA Modules:
  0.0 646.2 jit_solution(1695571141242845785)
XLA Ops:
  6.5 6.7 %stack.2 = bf16[256,32,1024]{2,1,0:T(8,128)(2,1)} broadcast(bf16[32,1024]{1,0:T(8,128)(2,1)} %param.15), dimensions={1,2} | broadcast | bytes 16842752 | tf_op jit(solution)/shard_map/stack | solution.py:16
  13.3 15.7 %all-to-all-start = ((bf16[256,32,1024]{2,1,0:T(8,128)(2,1)}), bf16[256,32,1024]{2,1,0:T(8,128)(2,1)}, u32[]{:S(2)}, u32[]{:S(2)}) async-start(bf16[256,32,1024]{2,1,0:T(8,128)(2,1)} %stack.2), calls=%async_computation | async-start | bytes 33554432 | tf_op jit(solution)/shard_map/all_to_all | solution.py:17
  31.1 8.2 %collective-permute-start = (bf16[24,24,1,128]{3,1,2,0:T(8,128)(2,1)S(1)}, bf16[24,24,1,128]{3,1,2,0:T(8,128)(2,1)S(1)}, u32[]{:S(2)}, u32[]{:S(2)}) collective-permute-start(bf16[24,24,1,128]{3,1,2,0:T(8,128)(2,1)S(1)} %get-tuple-element.9), channel_id=1, source_target_pairs={{0,1},{1,2},{2,3},{3,4},{4,5},{5,6},{6,7},{7,8},{8,9},{9,10},{10,1... | collective-permute-start | bytes 442376 | tf_op jit(solution)/shard_map/ppermute | solution.py:24
  39.4 4.5 collective-permute-start.1
  43.9 354.6 %collective-permute-done = bf16[24,24,1,128]{3,1,2,0:T(8,128)(2,1)S(1)} collective-permute-done((bf16[24,24,1,128]{3,1,2,0:T(8,128)(2,1)S(1)}, bf16[24,24,1,128]{3,1,2,0:T(8,128)(2,1)S(1)}, u32[]{:S(2)}, u32[]{:S(2)}) %collective-permute-start) | collective-permute-done | bytes 147488 | tf_op jit(solution)/shard_map/ppermute | solution.py:24
  398.6 6.9 %collective-permute-done.1 = bf16[24,24,1,128]{3,1,2,0:T(8,128)(2,1)S(1)} collective-permute-done((bf16[24,24,1,128]{3,1,2,0:T(8,128)(2,1)S(1)}, bf16[24,24,1,128]{3,1,2,0:T(8,128)(2,1)S(1)}, u32[]{:S(2)}, u32[]{:S(2)}) %collective-permute-start.1) | collective-permute-done | bytes 147488 | tf_op jit(solution)/shard_map/ppermute | solution.py:24
  405.8 3.4 collective-permute-start.2
  409.2 4.6 collective-permute-start.3
  420.2 4.2 collective-permute-start.4
  436.9 20.4 %copy.70 = bf16[12,12,12,3456]{3,2,1,0:T(8,128)(2,1)} copy(bf16[12,12,12,3456]{3,1,2,0:T(8,128)(2,1)S(1)} %slice_dynamic-update-slice_fusion) | data formatting | bytes 23887872 | tf_op jit(solution)/shard_map/concatenate | solution.py:49
  457.3 18.6 %reshape.97 = bf16[1728,3456]{1,0:T(8,128)(2,1)} reshape(bf16[12,12,12,3456]{3,2,1,0:T(8,128)(2,1)} %copy.70) | data formatting | bytes 23887872 | tf_op jit(solution)/shard_map/reshape | solution.py:58
  475.9 7.7 %multiply_convert_fusion = bf16[1728,128]{1,0:T(8,128)(2,1)S(1)} fusion(bf16[1728,3456]{1,0:T(8,128)(2,1)} %reshape.97, bf16[3456,128]{1,0:T(8,128)(2,1)S(1)} %bitcast.24, f32[128]{0:T(128)S(1)} %copy-done.5), kind=kOutput, calls=%fused_computation.14 | convolution fusion | flops 1530150912 | bytes 13271552 | tf_op jit(solution)/shard_map/dot_general | solution.py:59
  483.6 17.3 %copy.71 = bf16[3,4,3,4,3,4,128]{5,3,1,6,4,2,0:T(4,128)(2,1)} copy(bf16[3,4,3,4,3,4,128]{6,5,4,3,2,1,0:T(4,128)(2,1)S(1)} %bitcast.34) | data formatting | bytes 884736 | tf_op jit(solution)/shard_map/reshape;reshape | solution.py:67
  500.9 37.1 %reshape_stack_reshape.3 = bf16[27,8192]{1,0:T(8,128)(2,1)S(1)} reshape(bf16[3,3,3,128,4,4,4]{6,5,4,3,2,1,0:T(4,128)(2,1)} %bitcast.25) | data formatting | bytes 884736 | tf_op jit(solution)/shard_map/reshape;stack;reshape | solution.py:107
  538.0 8.8 %fusion.2 = bf16[27,1024]{1,0:T(8,128)(2,1)S(1)} fusion(bf16[27,8192]{1,0:T(8,128)(2,1)S(1)} %reshape_stack_reshape.3, bf16[8192,1024]{1,0:T(8,128)(2,1)} %bitcast.4, f32[1024]{0:T(1024)S(1)} %copy-done.2), kind=kOutput, calls=%fused_computation.13 | convolution fusion | flops 453040128 | bytes 17278976 | tf_op jit(solution)/shard_map/dot_general | solution.py:108
  546.8 9.0 %all_to_all.21 = bf16[27,8,128]{2,0,1:T(8,128)(2,1)S(1)} all-to-all(bf16[27,8,128]{2,0,1:T(8,128)(2,1)S(1)} %copy.72), channel_id=1, replica_groups=mesh['chan'=8,'region'=32] {'chan'}, dimensions={1} | all-to-all | bytes 110592 | tf_op jit(solution)/shard_map/all_to_all | solution.py:114
  556.0 4.2 collective-permute-start.6
  560.2 8.7 %collective-permute-start.7 = (bf16[2,6,6,1,128]{4,0,3,2,1:T(2,128)(2,1)S(1)}, bf16[2,6,6,1,128]{4,0,3,2,1:T(2,128)(2,1)S(1)}, u32[]{:S(2)}, u32[]{:S(2)}) collective-permute-start(bf16[2,6,6,1,128]{4,0,3,2,1:T(2,128)(2,1)S(1)} %get-tuple-element.48), channel_id=1, source_target_pairs={{1,0},{2,1},{3,2},{4,3},{5,4},{6,5},{7,6},{8,7},{9,8},{10,9},{11,1... | collective-permute-start | bytes 55304 | tf_op jit(solution)/shard_map/ppermute | solution.py:24
  570.5 3.2 collective-permute-start.8
  573.9 4.8 collective-permute-start.9
  580.5 3.6 collective-permute-start.10
  587.1 2.9 collective-permute-done.11
  593.3 5.8 fusion.16
  600.5 36.9 %reduce-scatter.2.cloned.1.call-done = f32[216,128]{1,0:T(8,128)} async-done(((f32[216,1024]{1,0:T(8,128)}), f32[216,128]{1,0:T(8,128)}) %reduce-scatter.2.cloned.1.call-update) | async-done | bytes 110608 | tf_op jit(solution)/shard_map/reduce_scatter | solution.py:133
  (170 shorter events, 32.8 us)
Async XLA Ops:
  6.5 469.4 %copy-start = (bf16[3,3,3,128,128]{4,3,2,1,0:T(8,128)(2,1)S(1)}, bf16[3,3,3,128,128]{4,3,2,1,0:T(8,128)(2,1)}, u32[]{:S(2)}) copy-start(bf16[3,3,3,128,128]{4,3,2,1,0:T(8,128)(2,1)} %param.13) | copy-start | bytes 2654212
  13.3 15.8 %copy-start.3 = (f32[128]{0:T(128)S(1)}, f32[128]{0:T(128)}, u32[]{:S(2)}) copy-start(f32[128]{0:T(128)} %param.12) | copy-start | bytes 1540
  13.3 15.8 %copy-start.4 = (f32[128]{0:T(128)S(1)}, f32[128]{0:T(128)}, u32[]{:S(2)}) copy-start(f32[128]{0:T(128)} %param.11) | copy-start | bytes 1540
  13.3 524.7 %all-to-all-start = ((bf16[256,32,1024]{2,1,0:T(8,128)(2,1)}), bf16[256,32,1024]{2,1,0:T(8,128)(2,1)}, u32[]{:S(2)}, u32[]{:S(2)}) async-start(bf16[256,32,1024]{2,1,0:T(8,128)(2,1)} %stack.2), calls=%async_computation | async-start | bytes 33554432 | tf_op jit(solution)/shard_map/all_to_all | solution.py:17
  29.0 608.5 %reduce-scatter.2.cloned.1.call-start = ((), (), s32[]{:S(2)}) async-start(), calls=%async_computation.3 | async-start | bytes 995328 | tf_op jit(solution)/shard_map/reduce_scatter | solution.py:133
  31.1 367.4 %collective-permute-start = (bf16[24,24,1,128]{3,1,2,0:T(8,128)(2,1)S(1)}, bf16[24,24,1,128]{3,1,2,0:T(8,128)(2,1)S(1)}, u32[]{:S(2)}, u32[]{:S(2)}) collective-permute-start(bf16[24,24,1,128]{3,1,2,0:T(8,128)(2,1)S(1)} %get-tuple-element.9), channel_id=1, source_target_pairs={{0,1},{1,2},{2,3},{3,4},{4,5},{5,6},{6,7},{7,8},{8,9},{9,10},{10,1... | collective-permute-start | bytes 442376 | tf_op jit(solution)/shard_map/ppermute | solution.py:24
  39.4 366.2 %collective-permute-start.1 = (bf16[24,24,1,128]{3,1,2,0:T(8,128)(2,1)S(1)}, bf16[24,24,1,128]{3,1,2,0:T(8,128)(2,1)S(1)}, u32[]{:S(2)}, u32[]{:S(2)}) collective-permute-start(bf16[24,24,1,128]{3,1,2,0:T(8,128)(2,1)S(1)} %get-tuple-element.10), channel_id=1, source_target_pairs={{1,0},{2,1},{3,2},{4,3},{5,4},{6,5},{7,6},{8,7},{9,8},{10,9},{11,1... | collective-permute-start | bytes 442376 | tf_op jit(solution)/shard_map/ppermute | solution.py:24
  405.8 10.1 %collective-permute-start.2 = (bf16[24,1,14,128]{3,1,2,0:T(2,128)(2,1)S(1)}, bf16[24,1,14,128]{3,1,2,0:T(2,128)(2,1)S(1)}, u32[]{:S(2)}, u32[]{:S(2)}) collective-permute-start(bf16[24,1,14,128]{3,1,2,0:T(2,128)(2,1)S(1)} %get-tuple-element.7), channel_id=1, source_target_pairs={{0,2},{1,3},{2,4},{3,5},{4,6},{5,7},{6,8},{7,9},{8,10},{9,11},{10,... | collective-permute-start | bytes 258056 | tf_op jit(solution)/shard_map/ppermute | solution.py:24
  409.2 8.0 %collective-permute-start.3 = (bf16[24,1,14,128]{3,1,2,0:T(2,128)(2,1)S(1)}, bf16[24,1,14,128]{3,1,2,0:T(2,128)(2,1)S(1)}, u32[]{:S(2)}, u32[]{:S(2)}) collective-permute-start(bf16[24,1,14,128]{3,1,2,0:T(2,128)(2,1)S(1)} %get-tuple-element.8), channel_id=1, source_target_pairs={{2,0},{3,1},{4,2},{5,3},{6,4},{7,5},{8,6},{9,7},{10,8},{11,9},{12,... | collective-permute-start | bytes 258056 | tf_op jit(solution)/shard_map/ppermute | solution.py:24
  418.1 6.9 %collective-permute-start.5 = (bf16[1,26,14,128]{3,1,2,0:T(8,128)(2,1)}, bf16[1,26,14,128]{3,1,2,0:T(8,128)(2,1)S(1)}, u32[]{:S(2)}, u32[]{:S(2)}) collective-permute-start(bf16[1,26,14,128]{3,1,2,0:T(8,128)(2,1)} %get-tuple-element.5), channel_id=1, source_target_pairs={{8,0},{9,1},{10,2},{11,3},{12,4},{13,5},{14,6},{15,7},{16,8},{17,9... | collective-permute-start | bytes 279560 | tf_op jit(solution)/shard_map/ppermute | solution.py:24
  420.2 6.7 %collective-permute-start.4 = (bf16[1,26,14,128]{3,1,2,0:T(8,128)(2,1)S(1)}, bf16[1,26,14,128]{3,1,2,0:T(8,128)(2,1)S(1)}, u32[]{:S(2)}, u32[]{:S(2)}) collective-permute-start(bf16[1,26,14,128]{3,1,2,0:T(8,128)(2,1)S(1)} %get-tuple-element.6), channel_id=1, source_target_pairs={{0,8},{1,9},{2,10},{3,11},{4,12},{5,13},{6,14},{7,15},{8,16},{9,17... | collective-permute-start | bytes 279560 | tf_op jit(solution)/shard_map/ppermute | solution.py:24
  457.3 18.6 %copy-start.5 = (f32[128]{0:T(128)S(1)}, f32[128]{0:T(128)}, u32[]{:S(2)}) copy-start(f32[128]{0:T(128)} %param.14) | copy-start | bytes 1540
  500.9 37.1 %copy-start.2 = (f32[1024]{0:T(1024)S(1)}, f32[1024]{0:T(1024)}, u32[]{:S(2)}) copy-start(f32[1024]{0:T(1024)} %param.16) | copy-start | bytes 12292
  556.0 13.0 %collective-permute-start.6 = (bf16[2,6,6,1,128]{4,0,3,2,1:T(2,128)(2,1)S(1)}, bf16[2,6,6,1,128]{4,0,3,2,1:T(2,128)(2,1)S(1)}, u32[]{:S(2)}, u32[]{:S(2)}) collective-permute-start(bf16[2,6,6,1,128]{4,0,3,2,1:T(2,128)(2,1)S(1)} %get-tuple-element.47), channel_id=1, source_target_pairs={{0,1},{1,2},{2,3},{3,4},{4,5},{5,6},{6,7},{7,8},{8,9},{9,10},{10,1... | collective-permute-start | bytes 55304 | tf_op jit(solution)/shard_map/ppermute | solution.py:24
  560.2 10.2 %collective-permute-start.7 = (bf16[2,6,6,1,128]{4,0,3,2,1:T(2,128)(2,1)S(1)}, bf16[2,6,6,1,128]{4,0,3,2,1:T(2,128)(2,1)S(1)}, u32[]{:S(2)}, u32[]{:S(2)}) collective-permute-start(bf16[2,6,6,1,128]{4,0,3,2,1:T(2,128)(2,1)S(1)} %get-tuple-element.48), channel_id=1, source_target_pairs={{1,0},{2,1},{3,2},{4,3},{5,4},{6,5},{7,6},{8,7},{9,8},{10,9},{11,1... | collective-permute-start | bytes 55304 | tf_op jit(solution)/shard_map/ppermute | solution.py:24
  570.5 8.3 %collective-permute-start.8 = (bf16[2,6,1,5,128]{4,0,3,2,1:T(2,128)(2,1)S(1)}, bf16[2,6,1,5,128]{4,0,3,2,1:T(2,128)(2,1)S(1)}, u32[]{:S(2)}, u32[]{:S(2)}) collective-permute-start(bf16[2,6,1,5,128]{4,0,3,2,1:T(2,128)(2,1)S(1)} %get-tuple-element.43), channel_id=1, source_target_pairs={{0,2},{1,3},{2,4},{3,5},{4,6},{5,7},{6,8},{7,9},{8,10},{9,11},{10,... | collective-permute-start | bytes 46088 | tf_op jit(solution)/shard_map/ppermute | solution.py:24
  573.9 6.2 collective-permute-start.9
  580.5 6.6 %collective-permute-start.10 = (bf16[2,1,8,5,128]{4,0,3,2,1:T(2,128)(2,1)S(1)}, bf16[2,1,8,5,128]{4,0,3,2,1:T(2,128)(2,1)S(1)}, u32[]{:S(2)}, u32[]{:S(2)}) collective-permute-start(bf16[2,1,8,5,128]{4,0,3,2,1:T(2,128)(2,1)S(1)} %get-tuple-element.32), channel_id=1, source_target_pairs={{0,8},{1,9},{2,10},{3,11},{4,12},{5,13},{6,14},{7,15},{8,16},{9,17... | collective-permute-start | bytes 61448 | tf_op jit(solution)/shard_map/ppermute | solution.py:24
  584.4 5.7 collective-permute-start.11
  593.3 45.8 %copy-start.1 = (bf16[3,3,3,128,128]{4,3,2,1,0:T(8,128)(2,1)S(1)}, bf16[3,3,3,128,128]{4,3,2,1,0:T(8,128)(2,1)}, u32[]{:S(2)}) copy-start(bf16[3,3,3,128,128]{4,3,2,1,0:T(8,128)(2,1)} %param.13) | copy-start | bytes 2654212
Sparse Core Ops, SparseCore 0:
  599.2 38.1 reduce-scatter.1
